TPU v7x, 256 devices: a whole 4x4x8 slice. The times are simulated.
256 devices in a mesh: dp: 8 (over x, core), graph: 32 (over y, z).
Axes of the slice: x: 4, y: 4, z: 8, core: 2. Of those that a mesh axis runs over, the one named last changes fastest.
Arguments:
- edges: bfloat16 [8, 65536, 1024], P('dp', 'graph'), may hold values from -6 to 6
- send_rows: int32 [8, 262144], P('dp', 'graph'), may hold values from 0 to 2047
- trip_src: int32 [8, 262144], P('dp', 'graph'), may hold values from 0 to 8191
- trip_dst: int32 [8, 262144], P('dp', 'graph'), may hold values from 0 to 2047
- basis_values: bfloat16 [8, 42, 262144], P('dp', None, 'graph'), may hold values from -6 to 6
- cotangent: bfloat16 [8, 65536, 1024], P('dp', 'graph'), may hold values from -6 to 6
- w_down: bfloat16 [1024, 128], replicated, may hold values from -0.1875 to 0.1875
- w_up: bfloat16 [128, 1024], replicated, may hold values from -0.5 to 0.5
- w_basis: bfloat16 [42, 128], replicated, may hold values from -1 to 1
Outputs:
- grad_edges: bfloat16 [8, 65536, 1024], P('dp', 'graph')
- grad_down: float32 [1024, 128], replicated
- grad_up: float32 [128, 1024], replicated
- grad_basis: float32 [42, 128], replicated
All inputs are finite; a program needn't handle non-finite values.
Results may differ from a plain program's by a relative error of at most 0.0073.
Values may be sent and summed in bfloat16 or wider, within the bound.
No kernel may reach another device: no remote copies, remote signals or barrier semaphores. Data moves between devices by JAX's collectives and lax.ppermute only.
A program may use at most 128 MiB of HBM per device.

v0:
```python
import jax
import jax.numpy as jnp
from jax import lax
from jax.sharding import PartitionSpec as P


def shards(edges, send_rows, trip_src, trip_dst, basis_values, cotangent, w_down, w_up, w_basis):
    edge_rows = edges[0]
    sendlist = send_rows[0]
    source_index = trip_src[0]
    target_index = trip_dst[0]
    basis_block = basis_values[0]
    grad_block = cotangent[0]
    local_edges = edge_rows.shape[0]
    down = jnp.dot(edge_rows, w_down, preferred_element_type=jnp.float32).astype(jnp.bfloat16)
    received = lax.all_to_all(
        jnp.take(down, sendlist, axis=0), "graph", split_axis=0, concat_axis=0, tiled=True
    )
    asked_rows = received.shape[0]
    source_rows = jnp.take(received, source_index, axis=0).astype(jnp.float32)
    basis_emb = lax.dot_general(
        basis_block, w_basis, (((0,), (0,)), ((), ())), preferred_element_type=jnp.float32
    )
    product = source_rows * basis_emb
    aggregate = jax.ops.segment_sum(product, target_index, num_segments=local_edges).astype(
        jnp.bfloat16
    )
    pre_act = jnp.dot(aggregate, w_up, preferred_element_type=jnp.float32)
    sigma = jax.nn.sigmoid(pre_act)
    g_pre = (grad_block.astype(jnp.float32) * sigma * (1.0 + pre_act * (1.0 - sigma))).astype(
        jnp.bfloat16
    )
    up_term = lax.dot_general(
        aggregate, g_pre, (((0,), (0,)), ((), ())), preferred_element_type=jnp.float32
    )
    g_agg = lax.dot_general(
        g_pre, w_up, (((1,), (1,)), ((), ())), preferred_element_type=jnp.float32
    )
    g_trip = jnp.take(g_agg, target_index, axis=0)
    g_source = g_trip * basis_emb
    g_basis_emb = g_trip * source_rows
    basis_term = jnp.dot(
        basis_block.astype(jnp.float32), g_basis_emb, precision=lax.Precision.HIGHEST
    )
    g_received = jax.ops.segment_sum(g_source, source_index, num_segments=asked_rows)
    returned = lax.all_to_all(g_received, "graph", split_axis=0, concat_axis=0, tiled=True)
    g_down = jax.ops.segment_sum(returned, sendlist, num_segments=local_edges).astype(jnp.bfloat16)
    grad_edges = lax.dot_general(
        g_down, w_down, (((1,), (1,)), ((), ())), preferred_element_type=jnp.float32
    )
    down_term = lax.dot_general(
        edge_rows, g_down, (((0,), (0,)), ((), ())), preferred_element_type=jnp.float32
    )
    grad_down, grad_up, grad_basis = lax.psum((down_term, up_term, basis_term), ("dp", "graph"))
    return (grad_edges.astype(jnp.bfloat16)[None], grad_down, grad_up, grad_basis)


def solution(mesh):
    in_specs = (
        P("dp", "graph", None),
        P("dp", "graph"),
        P("dp", "graph"),
        P("dp", "graph"),
        P("dp", None, "graph"),
        P("dp", "graph", None),
        P(),
        P(),
        P(),
    )
    out_specs = (P("dp", "graph", None), P(), P(), P())
    return jax.shard_map(shards, mesh=mesh, in_specs=in_specs, out_specs=out_specs, check_vma=False)
```

profile of v0, /device:TPU:2, one launch (start us, length us, event | category | flops | bytes accessed | tf_op | source)
XLA Modules:
  0.0 685.5 jit_solution(6888944162113069686)
XLA Ops:
  7.2 0.0 copy-start
  7.2 0.9 compare_select_fusion.2
  8.1 0.5 broadcast.107
  8.6 1.5 reduce.3
  10.1 3.5 fusion.12
  13.6 24.0 %gather_fusion = bf16[8192,128]{1,0:T(8,128)(2,1)S(1)} fusion(bf16[2048,128]{1,0:T(8,128)(2,1)S(1)} %fusion.12, s32[8192]{0:T(1024)S(1)} %broadcast_clamp_fusion.2), kind=kCustom, calls=%fused_computation | custom fusion | bytes 4227072 | tf_op jit(solution)/shard_map/jit(_take)/gather | solution.py:17
  37.6 0.0 copy-start.5
  37.6 0.0 copy-start.7
  37.7 2.7 broadcast_select_fusion.1
  40.3 11.5 %all-to-all-start = ((bf16[32,256,128]{2,1,0:T(8,128)(2,1)}), bf16[32,256,128]{2,1,0:T(8,128)(2,1)S(1)}, u32[]{:S(2)}, u32[]{:S(2)}) async-start(bf16[32,256,128]{2,1,0:T(8,128)(2,1)} %broadcast_select_fusion.1), calls=%async_computation | async-start | bytes 4194304 | tf_op jit(solution)/shard_map/all_to_all | solution.py:16
  52.0 2.8 fusion.25
  54.8 47.1 %all-to-all-done = bf16[32,256,128]{2,1,0:T(8,128)(2,1)S(1)} async-done(((bf16[32,256,128]{2,1,0:T(8,128)(2,1)}), bf16[32,256,128]{2,1,0:T(8,128)(2,1)S(1)}, u32[]{:S(2)}, u32[]{:S(2)}) %all-to-all-start) | async-done | bytes 2097184 | tf_op jit(solution)/shard_map/all_to_all | solution.py:16
  101.8 29.4 %gather_fusion.1 = bf16[8192,128]{1,0:T(8,128)(2,1)} fusion(bf16[8192,128]{1,0:T(8,128)(2,1)S(1)} %bitcast.46, s32[8192]{0:T(1024)S(1)} %broadcast_clamp_fusion), kind=kCustom, calls=%fused_computation.1 | custom fusion | bytes 4227072 | tf_op jit(solution)/shard_map/jit(_take)/gather | solution.py:20
  131.3 49.5 %scatter_custom_fusion = f32[2048,128]{1,0:T(8,128)S(1)} fusion(s32[8192]{0:T(1024)S(1)} %bitcast.50, f32[8192,128]{1,0:T(8,128)} %fusion.25, bf16[8192,128]{1,0:T(8,128)(2,1)} %gather_fusion.1, pred[8192]{0:T(1024)(128)(4,1)S(1)} %get-tuple-element.14, bf16[]{:T(256)} %constant.46.clone.1, f32[]{:T(128)} %constant.30.clone.1), kind=kCustom, calls=%fused_computation.11 | custom fusion | flops 4194304 | bytes 7348230 | tf_op jit(solution)/shard_map/scatter-add | solution.py:25
  180.8 5.7 fusion.1
  186.5 2.0 copy-done.1
  188.4 1.3 fusion.37
  189.7 27.8 %gather_fusion.2 = f32[8192,128]{1,0:T(8,128)} fusion(f32[2048,128]{1,0:T(8,128)S(1)} %fusion.37, s32[8192]{0:T(1024)S(1)} %broadcast_clamp_fusion.1), kind=kCustom, calls=%fused_computation.2 | custom fusion | bytes 8421376 | tf_op jit(solution)/shard_map/jit(_take)/gather | solution.py:39
  217.5 51.4 %scatter_custom_fusion.1 = f32[8192,128]{1,0:T(8,128)} fusion(s32[8192]{0:T(1024)S(1)} %bitcast.52, f32[8192,128]{1,0:T(8,128)} %fusion.25, f32[8192,128]{1,0:T(8,128)} %gather_fusion.2, f32[]{:T(128)} %constant.47.clone.1, f32[]{:T(128)} %constant.30.clone.1, pred[8192]{0:T(1024)(128)(4,1)S(1)} %get-tuple-element.15), kind=kCustom, calls=%fused_computation.18 | custom fusion | flops 3145728 | bytes 12591112 | tf_op jit(solution)/shard_map/scatter-add | solution.py:45
  269.0 6.3 all-to-all-start.1
  275.2 0.0 all-reduce.3.cloned.1.call-start
  275.3 3.7 fusion.32
  279.0 93.0 %all-to-all-done.1 = f32[32,256,128]{2,1,0:T(8,128)} async-done(((f32[32,256,128]{2,1,0:T(8,128)}), f32[32,256,128]{2,1,0:T(8,128)}, u32[]{:S(2)}, u32[]{:S(2)}) %all-to-all-start.1) | async-done | bytes 4194336 | tf_op jit(solution)/shard_map/all_to_all | solution.py:46
  372.0 45.4 %scatter_custom_fusion.2 = f32[2048,128]{1,0:T(8,128)} fusion(s32[8192]{0:T(1024)} %bitcast.53, f32[8192,128]{1,0:T(8,128)} %bitcast.15, f32[]{:T(128)} %constant.30.clone.1), kind=kCustom, calls=%fused_computation.35 | custom fusion | flops 1048576 | bytes 1049088 | tf_op jit(solution)/shard_map/scatter-add | solution.py:47
  417.4 4.0 fusion.20
  421.4 0.0 all-reduce.3.cloned.1.call-update
  421.4 7.1 %fusion.23 = f32[42,128]{1,0:T(8,128)S(1)} fusion(f32[8192,128]{1,0:T(8,128)} %gather_fusion.2, pred[8192]{0:T(1024)(128)(4,1)S(1)} %get-tuple-element.15, bf16[8192,128]{1,0:T(8,128)(2,1)S(1)} %copy-done.2, pred[8192]{0:T(1024)(128)(4,1)S(1)} %get-tuple-element.14, bf16[1,42,8192]{2,1,0:T(8,128)(2,1)S(1)} %copy-done), kind=kOutput, calls=%fused_computation.31 | convolution fusion | flops 532676608 | bytes 7017472 | tf_op jit(solution)/shard_map/dot_general | solution.py:42
  428.5 74.3 %psum.23 = f32[42,128]{1,0:T(8,128)} all-reduce(f32[42,128]{1,0:T(8,128)S(1)} %fusion.23), channel_id=1, replica_groups=mesh['dp'=8,'graph'=32] {'dp','graph'}, use_global_device_ids=true, to_apply=%region_5.6 | all-reduce | flops 5376 | bytes 43008 | tf_op jit(solution)/shard_map/psum | solution.py:54
  502.8 4.5 convert_bitcast_fusion
  507.3 167.4 %all-reduce.3.cloned.1.call-done = (f32[1024,128]{0,1:T(8,128)}, f32[128,1024]{1,0:T(8,128)}) async-done(((f32[1024,128]{0,1:T(8,128)}, f32[128,1024]{1,0:T(8,128)}), (f32[1024,128]{0,1:T(8,128)}, f32[128,1024]{1,0:T(8,128)})) %all-reduce.3.cloned.1.call-update) | async-done | bytes 1048592 | tf_op jit(solution)/shard_map/psum | solution.py:54
  674.7 2.0 copy.14
  676.7 1.9 copy.17
  (20 shorter events, 0.2 us)
Async XLA Ops:
  7.2 44.8 %copy-start = (bf16[1,42,8192]{2,1,0:T(8,128)(2,1)S(1)}, bf16[1,42,8192]{2,1,0:T(8,128)(2,1)}, u32[]{:S(2)}) copy-start(bf16[1,42,8192]{2,1,0:T(8,128)(2,1)} %param.13) | copy-start | bytes 2064388
  37.6 14.2 %copy-start.6 = (s32[1,8192]{1,0:T(1,128)S(1)}, s32[1,8192]{1,0:T(1,128)}, u32[]{:S(2)}) copy-start(s32[1,8192]{1,0:T(1,128)} %param.11) | copy-start | bytes 98308
  37.6 14.3 %copy-start.5 = (s32[1,8192]{1,0:T(1,128)S(1)}, s32[1,8192]{1,0:T(1,128)}, u32[]{:S(2)}) copy-start(s32[1,8192]{1,0:T(1,128)} %param.12) | copy-start | bytes 98308
  37.6 14.4 %copy-start.7 = (bf16[42,128]{1,0:T(8,128)(2,1)S(1)}, bf16[42,128]{1,0:T(8,128)(2,1)}, u32[]{:S(2)}) copy-start(bf16[42,128]{1,0:T(8,128)(2,1)} %param.17) | copy-start | bytes 32260
  40.3 61.5 %all-to-all-start = ((bf16[32,256,128]{2,1,0:T(8,128)(2,1)}), bf16[32,256,128]{2,1,0:T(8,128)(2,1)S(1)}, u32[]{:S(2)}, u32[]{:S(2)}) async-start(bf16[32,256,128]{2,1,0:T(8,128)(2,1)} %broadcast_select_fusion.1), calls=%async_computation | async-start | bytes 4194304 | tf_op jit(solution)/shard_map/all_to_all | solution.py:16
  131.3 49.5 %copy-start.3 = (bf16[128,1024]{1,0:T(8,128)(2,1)S(1)}, bf16[128,1024]{1,0:T(8,128)(2,1)}, u32[]{:S(2)}) copy-start(bf16[128,1024]{1,0:T(8,128)(2,1)} %param.16) | copy-start | bytes 786436
  186.5 2.0 copy-start.1
  269.0 103.0 %all-to-all-start.1 = ((f32[32,256,128]{2,1,0:T(8,128)}), f32[32,256,128]{2,1,0:T(8,128)}, u32[]{:S(2)}, u32[]{:S(2)}) async-start(f32[32,256,128]{2,1,0:T(8,128)} %bitcast.47), calls=%async_computation.1 | async-start | bytes 8388608 | tf_op jit(solution)/shard_map/all_to_all | solution.py:46
  275.2 399.5 %all-reduce.3.cloned.1.call-start = ((), (), s32[]{:S(2)}) async-start(), calls=%async_computation.2 | async-start | bytes 2097152 | tf_op jit(solution)/shard_map/psum | solution.py:54
  279.0 142.4 %copy-start.2 = (bf16[8192,128]{1,0:T(8,128)(2,1)S(1)}, bf16[8192,128]{1,0:T(8,128)(2,1)}, u32[]{:S(2)}) copy-start(bf16[8192,128]{1,0:T(8,128)(2,1)} %gather_fusion.1) | copy-start | bytes 6291460
  421.4 81.4 %copy-start.4 = (bf16[1024,128]{1,0:T(8,128)(2,1)S(1)}, bf16[1024,128]{1,0:T(8,128)(2,1)}, u32[]{:S(2)}) copy-start(bf16[1024,128]{1,0:T(8,128)(2,1)} %param.15) | copy-start | bytes 786436
Sparse Core Ops, SparseCore 0:
  421.6 253.1 all-reduce.2
where the time goes:
time: 686 us; the launch traced here: 685 us
  waiting for transfers between devices  307 us (45%)
  other arithmetic  151 us (22%)
  local copies, waits for them, and re-layouts  87.8 us (13%)
  blocking collectives  74.3 us (11%)
  matrix products  32.5 us (5%)
  starting transfers between devices  17.8 us (3%)
  between operations  14.3 us (2%)
    psum x1, waiting for transfers between devices, shards(): lax.psum((down_term, up_term, basis_term), ('dp', 'graph'))  167 us
    all_to_all x1, waiting for transfers between devices, shards(): lax.all_to_all(g_received, 'graph', split_axis=0, concat_axis=0, tiled=True)  93 us
    psum x1, blocking collectives, shards(): lax.psum((down_term, up_term, basis_term), ('dp', 'graph'))  74.3 us
    scatter-add x1, other arithmetic, shards(): jax.ops.segment_sum(g_source, source_index, num_segments=asked_rows)  51.4 us
    scatter-add x1, other arithmetic, shards(): jax.ops.segment_sum(product, target_index, num_segments=local_edges)  49.5 us
    all_to_all x1, waiting for transfers between devices, shards(): lax.all_to_all(jnp.take(down, sendlist, axis=0), 'graph', split_axis=0, c...  47.1 us
    scatter-add x1, other arithmetic, shards(): jax.ops.segment_sum(returned, sendlist, num_segments=local_edges)  45.4 us
    gather x1, local copies, waits for them, and re-layouts, shards(): source_rows = jnp.take(received, source_index, axis=0).astype(jnp.float32)  29.4 us
  transfers between devices with their start and end apart: 3, of which 3 were waited for; matrix products, arithmetic and copies ran while one was open for 3% of the time, Pallas kernels for 0%

commit v1 on v0

--- a/solution.py
+++ b/solution.py
@@ -2,6 +2,8 @@
 import jax.numpy as jnp
 from jax import lax
 from jax.sharding import PartitionSpec as P
+
+order_the_clusters = lambda v0: jax.lax.psum(jax.lax.psum(v0, "graph"), "dp")
 
 
 def shards(edges, send_rows, trip_src, trip_dst, basis_values, cotangent, w_down, w_up, w_basis):
@@ -51,7 +53,7 @@
     down_term = lax.dot_general(
         edge_rows, g_down, (((0,), (0,)), ((), ())), preferred_element_type=jnp.float32
     )
-    grad_down, grad_up, grad_basis = lax.psum((down_term, up_term, basis_term), ("dp", "graph"))
+    grad_down, grad_up, grad_basis = order_the_clusters((down_term, up_term, basis_term))
     return (grad_edges.astype(jnp.bfloat16)[None], grad_down, grad_up, grad_basis)
 
 

time: 686 us -> 753 us (1.098)
  blocking collectives: 74.3 us -> 162 us
  waiting for transfers between devices: 307 us -> 286 us
    psum x1 -> x2, blocking collectives: 74.3 us -> 162 us  [the longest x1 140 us: jax.lax.psum(v0, 'graph')]
    psum x1 -> x2, waiting for transfers between devices: 167 us -> 146 us  [the longest x1 146 us: jax.lax.psum(v0, 'graph')]
  transfers between devices with their start and end apart: 3 -> 4, of which waited for: 3 -> 3; matrix products, arithmetic and copies ran while one was open for 3% -> 2% of each run, Pallas kernels for 0% -> 0%
where the time goes in v1:
time: 753 us; the launch traced here: 752 us
  waiting for transfers between devices  286 us (38%)
  blocking collectives  162 us (22%)
  other arithmetic  151 us (20%)
  local copies, waits for them, and re-layouts  87.4 us (12%)
  matrix products  32.6 us (4%)
  starting transfers between devices  17.8 us (2%)
  between operations  14.3 us (2%)
    psum x1, waiting for transfers between devices, jax.lax.psum(v0, 'graph')  146 us
    psum x1, blocking collectives, jax.lax.psum(v0, 'graph')  140 us
    all_to_all x1, waiting for transfers between devices, shards(): lax.all_to_all(g_received, 'graph', split_axis=0, concat_axis=0, tiled=True)  93 us
    scatter-add x1, other arithmetic, shards(): jax.ops.segment_sum(g_source, source_index, num_segments=asked_rows)  51.4 us
    scatter-add x1, other arithmetic, shards(): jax.ops.segment_sum(product, target_index, num_segments=local_edges)  49.5 us
    all_to_all x1, waiting for transfers between devices, shards(): lax.all_to_all(jnp.take(down, sendlist, axis=0), 'graph', split_axis=0, c...  47.1 us
    scatter-add x1, other arithmetic, shards(): jax.ops.segment_sum(returned, sendlist, num_segments=local_edges)  45.4 us
    gather x1, local copies, waits for them, and re-layouts, shards(): source_rows = jnp.take(received, source_index, axis=0).astype(jnp.float32)  29.2 us
  transfers between devices with their start and end apart: 4, of which 3 were waited for; matrix products, arithmetic and copies ran while one was open for 2% of the time, Pallas kernels for 0%

profile of v1, /device:TPU:2, one launch (start us, length us, event | category | flops | bytes accessed | tf_op | source)
XLA Modules:
  0.0 751.6 jit_solution(10304434281487639470)
XLA Ops:
  7.2 0.9 compare_select_fusion.2
  8.1 0.5 broadcast.107
  8.6 1.5 reduce.3
  10.1 3.5 fusion.12
  13.6 24.0 %gather_fusion = bf16[8192,128]{1,0:T(8,128)(2,1)S(1)} fusion(bf16[2048,128]{1,0:T(8,128)(2,1)S(1)} %fusion.12, s32[8192]{0:T(1024)S(1)} %broadcast_clamp_fusion.2), kind=kCustom, calls=%fused_computation | custom fusion | bytes 4227072 | tf_op jit(solution)/shard_map/jit(_take)/gather | solution.py:19
  37.7 2.7 broadcast_select_fusion.1
  40.3 11.5 %all-to-all-start = ((bf16[32,256,128]{2,1,0:T(8,128)(2,1)}), bf16[32,256,128]{2,1,0:T(8,128)(2,1)S(1)}, u32[]{:S(2)}, u32[]{:S(2)}) async-start(bf16[32,256,128]{2,1,0:T(8,128)(2,1)} %broadcast_select_fusion.1), calls=%async_computation | async-start | bytes 4194304 | tf_op jit(solution)/shard_map/all_to_all | solution.py:18
  52.0 2.8 fusion.25
  54.8 47.1 %all-to-all-done = bf16[32,256,128]{2,1,0:T(8,128)(2,1)S(1)} async-done(((bf16[32,256,128]{2,1,0:T(8,128)(2,1)}), bf16[32,256,128]{2,1,0:T(8,128)(2,1)S(1)}, u32[]{:S(2)}, u32[]{:S(2)}) %all-to-all-start) | async-done | bytes 2097184 | tf_op jit(solution)/shard_map/all_to_all | solution.py:18
  101.9 29.2 %gather_fusion.1 = bf16[8192,128]{1,0:T(8,128)(2,1)} fusion(bf16[8192,128]{1,0:T(8,128)(2,1)S(1)} %bitcast.46, s32[8192]{0:T(1024)S(1)} %broadcast_clamp_fusion), kind=kCustom, calls=%fused_computation.1 | custom fusion | bytes 4227072 | tf_op jit(solution)/shard_map/jit(_take)/gather | solution.py:22
  131.1 49.5 %scatter_custom_fusion = f32[2048,128]{1,0:T(8,128)S(1)} fusion(s32[8192]{0:T(1024)S(1)} %bitcast.50, f32[8192,128]{1,0:T(8,128)} %fusion.25, bf16[8192,128]{1,0:T(8,128)(2,1)} %gather_fusion.1, pred[8192]{0:T(1024)(128)(4,1)S(1)} %get-tuple-element.16, bf16[]{:T(256)} %constant.46.clone.1, f32[]{:T(128)} %constant.30.clone.1), kind=kCustom, calls=%fused_computation.11 | custom fusion | flops 4194304 | bytes 7348230 | tf_op jit(solution)/shard_map/scatter-add | solution.py:27
  180.6 5.7 fusion.1
  186.3 2.0 copy-done.1
  188.2 1.2 fusion.37
  189.5 27.7 %gather_fusion.2 = f32[8192,128]{1,0:T(8,128)} fusion(f32[2048,128]{1,0:T(8,128)S(1)} %fusion.37, s32[8192]{0:T(1024)S(1)} %broadcast_clamp_fusion.1), kind=kCustom, calls=%fused_computation.2 | custom fusion | bytes 8421376 | tf_op jit(solution)/shard_map/jit(_take)/gather | solution.py:41
  217.2 51.4 %scatter_custom_fusion.1 = f32[8192,128]{1,0:T(8,128)} fusion(s32[8192]{0:T(1024)S(1)} %bitcast.52, f32[8192,128]{1,0:T(8,128)} %fusion.25, f32[8192,128]{1,0:T(8,128)} %gather_fusion.2, f32[]{:T(128)} %constant.47.clone.1, f32[]{:T(128)} %constant.30.clone.1, pred[8192]{0:T(1024)(128)(4,1)S(1)} %get-tuple-element.17), kind=kCustom, calls=%fused_computation.18 | custom fusion | flops 3145728 | bytes 12591112 | tf_op jit(solution)/shard_map/scatter-add | solution.py:47
  268.6 6.3 all-to-all-start.1
  274.9 0.0 all-reduce.5.cloned.1.call-start
  274.9 3.7 fusion.32
  278.7 93.0 %all-to-all-done.1 = f32[32,256,128]{2,1,0:T(8,128)} async-done(((f32[32,256,128]{2,1,0:T(8,128)}), f32[32,256,128]{2,1,0:T(8,128)}, u32[]{:S(2)}, u32[]{:S(2)}) %all-to-all-start.1) | async-done | bytes 4194336 | tf_op jit(solution)/shard_map/all_to_all | solution.py:48
  371.6 45.4 %scatter_custom_fusion.2 = f32[2048,128]{1,0:T(8,128)} fusion(s32[8192]{0:T(1024)} %bitcast.53, f32[8192,128]{1,0:T(8,128)} %bitcast.15, f32[]{:T(128)} %constant.30.clone.1), kind=kCustom, calls=%fused_computation.35 | custom fusion | flops 1048576 | bytes 1049088 | tf_op jit(solution)/shard_map/scatter-add | solution.py:49
  417.0 4.2 fusion.20
  421.2 0.0 all-reduce.5.cloned.1.call-update
  421.2 0.0 all-reduce.7.cloned.1.call-start
  421.3 146.2 %all-reduce.5.cloned.1.call-done = (f32[1024,128]{0,1:T(8,128)}, f32[128,1024]{1,0:T(8,128)}) async-done(((f32[1024,128]{0,1:T(8,128)}, f32[128,1024]{1,0:T(8,128)}), (f32[1024,128]{0,1:T(8,128)}, f32[128,1024]{1,0:T(8,128)})) %all-reduce.5.cloned.1.call-update) | async-done | bytes 1048592 | tf_op jit(solution)/shard_map/psum | solution.py:6
  567.5 0.0 all-reduce.7.cloned.1.call-update
  567.6 7.0 fusion.23
  574.6 140.4 %psum.46 = f32[42,128]{1,0:T(8,128)S(1)} all-reduce(f32[42,128]{1,0:T(8,128)S(1)} %fusion.23), channel_id=1, replica_groups=mesh['dp'=8,'graph'=32] {'graph'}, use_global_device_ids=true, to_apply=%region_7.8 | all-reduce | flops 5376 | bytes 43008 | tf_op jit(solution)/shard_map/psum | solution.py:6
  715.0 21.3 %psum.47 = f32[42,128]{1,0:T(8,128)} all-reduce(f32[42,128]{1,0:T(8,128)S(1)} %psum.46), channel_id=1, replica_groups=mesh['dp'=8,'graph'=32] {'dp'}, use_global_device_ids=true, to_apply=%region_8.9 | all-reduce | flops 5376 | bytes 43008 | tf_op jit(solution)/shard_map/psum | solution.py:6
  736.3 4.5 convert_bitcast_fusion
  740.8 2.0 copy.14
  742.8 1.9 copy.19
  (24 shorter events, 0.2 us)
Async XLA Ops:
  7.2 44.8 %copy-start = (bf16[1,42,8192]{2,1,0:T(8,128)(2,1)S(1)}, bf16[1,42,8192]{2,1,0:T(8,128)(2,1)}, u32[]{:S(2)}) copy-start(bf16[1,42,8192]{2,1,0:T(8,128)(2,1)} %param.13) | copy-start | bytes 2064388
  37.6 14.2 %copy-start.6 = (s32[1,8192]{1,0:T(1,128)S(1)}, s32[1,8192]{1,0:T(1,128)}, u32[]{:S(2)}) copy-start(s32[1,8192]{1,0:T(1,128)} %param.11) | copy-start | bytes 98308
  37.6 14.3 %copy-start.5 = (s32[1,8192]{1,0:T(1,128)S(1)}, s32[1,8192]{1,0:T(1,128)}, u32[]{:S(2)}) copy-start(s32[1,8192]{1,0:T(1,128)} %param.12) | copy-start | bytes 98308
  37.6 14.4 %copy-start.7 = (bf16[42,128]{1,0:T(8,128)(2,1)S(1)}, bf16[42,128]{1,0:T(8,128)(2,1)}, u32[]{:S(2)}) copy-start(bf16[42,128]{1,0:T(8,128)(2,1)} %param.17) | copy-start | bytes 32260
  40.3 61.5 %all-to-all-start = ((bf16[32,256,128]{2,1,0:T(8,128)(2,1)}), bf16[32,256,128]{2,1,0:T(8,128)(2,1)S(1)}, u32[]{:S(2)}, u32[]{:S(2)}) async-start(bf16[32,256,128]{2,1,0:T(8,128)(2,1)} %broadcast_select_fusion.1), calls=%async_computation | async-start | bytes 4194304 | tf_op jit(solution)/shard_map/all_to_all | solution.py:18
  131.1 49.5 %copy-start.3 = (bf16[128,1024]{1,0:T(8,128)(2,1)S(1)}, bf16[128,1024]{1,0:T(8,128)(2,1)}, u32[]{:S(2)}) copy-start(bf16[128,1024]{1,0:T(8,128)(2,1)} %param.16) | copy-start | bytes 786436
  186.3 2.0 copy-start.1
  268.6 103.0 %all-to-all-start.1 = ((f32[32,256,128]{2,1,0:T(8,128)}), f32[32,256,128]{2,1,0:T(8,128)}, u32[]{:S(2)}, u32[]{:S(2)}) async-start(f32[32,256,128]{2,1,0:T(8,128)} %bitcast.47), calls=%async_computation.1 | async-start | bytes 8388608 | tf_op jit(solution)/shard_map/all_to_all | solution.py:48
  274.9 292.6 %all-reduce.5.cloned.1.call-start = ((), (), s32[]{:S(2)}) async-start(), calls=%async_computation.2 | async-start | bytes 2097152 | tf_op jit(solution)/shard_map/psum | solution.py:6
  417.0 150.6 %copy-start.2 = (bf16[8192,128]{1,0:T(8,128)(2,1)S(1)}, bf16[8192,128]{1,0:T(8,128)(2,1)}, u32[]{:S(2)}) copy-start(bf16[8192,128]{1,0:T(8,128)(2,1)} %gather_fusion.1) | copy-start | bytes 6291460
  421.2 315.1 %copy-start.4 = (bf16[1024,128]{1,0:T(8,128)(2,1)S(1)}, bf16[1024,128]{1,0:T(8,128)(2,1)}, u32[]{:S(2)}) copy-start(bf16[1024,128]{1,0:T(8,128)(2,1)} %param.15) | copy-start | bytes 786436
  421.2 319.5 %all-reduce.7.cloned.1.call-start = ((), (), s32[]{:S(2)}) async-start(), calls=%async_computation.3 | async-start | bytes 2097152 | tf_op jit(solution)/shard_map/psum | solution.py:6
Sparse Core Ops, SparseCore 0:
  421.4 146.1 all-reduce.4
  570.0 62.9 all-reduce.6
